TPU v7x, 32 devices: a whole 2x2x4 slice. The times are simulated.
32 devices in a mesh: owner: 16 (over z, y, x), replica: 2 (over core).
Axes of the slice: x: 2, y: 2, z: 4, core: 2. Of those that a mesh axis runs over, the one named last changes fastest.
Arguments:
- queries: bfloat16 [256, 32, 128], P(('owner', 'replica')), may hold values from -8 to 8
- pages: bfloat16 [16, 1024, 128], P('owner'), may hold values from -3 to 3
- pair_page: int32 [2048, 1], P(('owner', 'replica')), may hold values from 0 to 15, as said below
- pair_query: int32 [2048], P(('owner', 'replica')), may hold values from 0 to 7
- pair_label: int32 [2048], P(('owner', 'replica')), may hold values 0 or 1
- hot_pages: int32 [2], replicated, may hold values from 0 to 15, as said below
Outputs:
- query_grad: bfloat16 [256, 32, 128], P(('owner', 'replica'))
- page_grad: bfloat16 [16, 1024, 128], P('owner', 'replica')
Inputs may be any that keep to these rules, and one draw needn't show every extreme that they name: `pair_page`: the rows of one device name no page more than 16 times, and some page exactly 16 times. `hot_pages`: 2 different page numbers; the last page is always among them.
All inputs are finite; a program needn't handle non-finite values. No bound on the sum of `pair_label` on one device may be relied on, other than what follows from the above.
Results may differ from a plain program's by a relative error of at most 0.0085.
Values may be sent and summed in bfloat16 or wider, within the bound.
A program may use at most 64 MiB of HBM per device.

v0:
```python
import functools
import math

import jax
import jax.numpy as jnp
from jax import lax
from jax.experimental import pallas as pl
from jax.experimental.pallas import tpu as pltpu
from jax.sharding import PartitionSpec as P

MESH = pl.DeviceIdType.MESH


def dense_kernel(
    lines,
    planes,
    shapes,
    query_ref,
    page_ref,
    pair_page_ref,
    pair_query_ref,
    pair_label_ref,
    hot_ref,
    query_grad_ref,
    page_grad_ref,
    held,
    paged,
    page_acc,
    query_acc,
    page_rows,
    swap_out,
    swap_in,
    share_out,
    share_in,
    part_out,
    part_in,
    line_sem,
    line_in_sem,
    plane_sem,
    plane_in_sem,
    relay_sem,
    relay_in_sem,
    swap_sem,
    swap_in_sem,
    share_sem,
    share_in_sem,
    part_sem,
    part_in_sem,
):
    local_queries, tokens_each, width, patches = shapes
    rows = local_queries * tokens_each
    flag_rows = held.shape[1] - rows
    part = patches // 2
    me = lax.axis_index("owner")
    core = lax.axis_index("replica")

    my_line, my_plane = me // planes, me % planes

    barrier = pltpu.get_barrier_semaphore()

    def greet(owner):
        pl.semaphore_signal(barrier, inc=1, device_id={"owner": owner}, device_id_type=MESH)

    for step in range(1, lines):
        greet((my_line ^ step) * planes + my_plane)
    for step in range(1, planes):
        greet(my_line * planes + (my_plane ^ step))
    pl.semaphore_signal(barrier, inc=1, device_id={"replica": 1 - core}, device_id_type=MESH)

    pairs = pair_page_ref.shape[1]
    lanes = held.shape[2]
    page_hot = (
        lax.broadcasted_iota(jnp.int32, (lanes, pairs), 0) == pair_page_ref[...]
    ).astype(jnp.float32)
    query_hot = lax.broadcasted_iota(jnp.int32, (local_queries, pairs), 0) == pair_query_ref[...]
    counted = query_hot.astype(jnp.float32)
    labelled = counted * pair_label_ref[...].astype(jnp.float32)
    stacked = jnp.concatenate([counted, labelled], axis=0)
    flags = lax.dot_general(
        stacked, page_hot, (((1,), (1,)), ((), ())), preferred_element_type=jnp.float32
    )
    held[my_line, pl.ds(0, rows), :] = query_ref[...]
    held[my_line, pl.ds(rows, flag_rows), :] = flags.astype(jnp.bfloat16)

    offset = -0.5 * tokens_each * (math.log(patches) / 4.0 + 2.0)

    row_query = lax.broadcasted_iota(jnp.int32, (rows, flag_rows), 0) // tokens_each
    flag_row = lax.broadcasted_iota(jnp.int32, (rows, flag_rows), 1)
    count_pick = (flag_row == row_query).astype(jnp.bfloat16)
    label_pick = (flag_row == row_query + local_queries).astype(jnp.bfloat16)
    lane = lax.broadcasted_iota(jnp.int32, (1, lanes), 1)

    paged[my_plane] = page_ref[...].reshape(paged.shape[1:])
    page_acc[...] = jnp.zeros_like(page_acc)
    query_acc[...] = jnp.zeros_like(query_acc)
    scale = 4.0 * math.log2(math.e)

    def logits(line, plane):
        tokens = held[line, pl.ds(0, rows), :]
        return lax.dot_general(
            tokens,
            paged[plane].reshape(patches, width),
            (((1,), (1,)), ((), ())),
            preferred_element_type=jnp.float32,
        )

    def weights(dots, line, plane):
        page = my_line * planes + plane
        own_lane = (lane == page).astype(jnp.float32)
        own_shift = 2.0 * jnp.sum((hot_ref[...] == page).astype(jnp.float32), keepdims=True)
        flag = held[line, pl.ds(rows, flag_rows), :]
        counts = jnp.sum(
            jnp.dot(count_pick, flag, preferred_element_type=jnp.float32) * own_lane,
            axis=1,
            keepdims=True,
        )
        labels = jnp.sum(
            jnp.dot(label_pick, flag, preferred_element_type=jnp.float32) * own_lane,
            axis=1,
            keepdims=True,
        )
        peak = jnp.max(dots, axis=1, keepdims=True)
        expo = jnp.exp2((dots - peak) * scale)
        totals = jnp.sum(expo, axis=1, keepdims=True)
        log_total = 4.0 * peak + jnp.log(totals)
        score = jnp.sum(log_total.reshape(local_queries, tokens_each, 1), axis=1, keepdims=True)
        score = jnp.broadcast_to(score, (local_queries, tokens_each, 1)).reshape(rows, 1)
        logit = 0.5 * (score / 4.0) + offset - own_shift
        slope = 0.5 * (counts * jax.nn.sigmoid(logit) - labels)
        return (expo * (slope / totals)).astype(jnp.bfloat16)

    def gradients(weight, line, plane):
        tokens = held[line, pl.ds(0, rows), :]
        query_acc[line] += jnp.dot(
            weight, paged[plane].reshape(patches, width), preferred_element_type=jnp.float32
        )
        page_acc[plane] += lax.dot_general(
            tokens, weight, (((0,), (0,)), ((), ())), preferred_element_type=jnp.float32
        )

    def block(*lines_of, plane):
        dots = [logits(line, plane) for line in lines_of]
        for line, dot in zip(lines_of, dots):
            gradients(weights(dot, line, plane), line, plane)

    block(my_line, plane=my_plane)
    pl.semaphore_wait(barrier, lines + planes - 1)

    def remote(src, dst, sent, received, device):
        return pltpu.make_async_remote_copy(
            src_ref=src,
            dst_ref=dst,
            send_sem=sent,
            recv_sem=received,
            device_id=device,
            device_id_type=MESH,
        )

    def to_line(line):
        return {"owner": line * planes + my_plane}

    def to_plane(plane):
        return {"owner": my_line * planes + plane}

    twin = {"replica": 1 - core}

    def tokens_to(line):
        slot = held.at[my_line]
        return remote(slot, slot, line_sem.at[line], line_in_sem.at[my_line], to_line(line))

    def tokens_from(line):
        slot = held.at[line]
        return remote(slot, slot, line_sem.at[line], line_in_sem.at[line], to_line(line))

    def page_to(plane):
        src = page_ref.at[pl.ds(core * part, part), :]
        dst = paged.at[my_plane, core]
        return remote(src, dst, plane_sem.at[plane], plane_in_sem.at[my_plane], to_plane(plane))

    def page_from(plane):
        slot = paged.at[plane, core]
        return remote(slot, slot, plane_sem.at[plane], plane_in_sem.at[plane], to_plane(plane))

    def relay(plane):
        slot = paged.at[plane, core]
        return remote(slot, slot, relay_sem.at[plane], relay_in_sem.at[plane], twin)

    def relayed(plane):
        slot = paged.at[plane, 1 - core]
        return remote(slot, slot, relay_sem.at[plane], relay_in_sem.at[plane], twin)

    def swap(plane):
        return remote(
            swap_out.at[plane], swap_in.at[plane], swap_sem.at[plane], swap_in_sem.at[plane], twin
        )

    def share_to(plane):
        dst = share_in.at[my_plane]
        sent, received = share_sem.at[plane], share_in_sem.at[my_plane]
        return remote(share_out.at[plane], dst, sent, received, to_plane(plane))

    def share_from(plane):
        dst = share_in.at[plane]
        sent, received = share_sem.at[plane], share_in_sem.at[plane]
        return remote(share_out.at[plane], dst, sent, received, to_plane(plane))

    def part_to(line):
        dst = part_in.at[my_line]
        sent, received = part_sem.at[line], part_in_sem.at[my_line]
        return remote(part_out.at[line], dst, sent, received, to_line(line))

    def part_from(line):
        dst = part_in.at[line]
        sent, received = part_sem.at[line], part_in_sem.at[line]
        return remote(part_out.at[line], dst, sent, received, to_line(line))

    for step in range(1, max(lines, planes)):
        if step < planes:
            page_to(my_plane ^ step).start()
        if step < lines:
            tokens_to(my_line ^ step).start()

    def finish_line(line):
        part_out[line] = query_acc[line].astype(jnp.bfloat16)
        part_to(line).start()

    def finish_page(plane):
        page_rows[plane] = page_acc[plane].T.reshape(page_rows.shape[1:])
        swap_out[plane] = page_rows[plane, 1 - core].astype(jnp.bfloat16)
        swap(plane).start()

    def half_page(plane):
        swap(plane).wait_recv()
        return page_rows[plane, core] + swap_in[plane].astype(jnp.float32)

    def share_page(plane):
        share_out[plane] = half_page(plane).astype(jnp.bfloat16)
        share_to(plane).start()

    def own_page(step, carry):
        line = my_line ^ step
        tokens_from(line).wait_recv()
        block(line, plane=my_plane)

        @pl.when(step < planes)
        def _():
            page_from(my_plane ^ step).wait_recv()
            relay(my_plane ^ step).start()

        return carry

    lax.fori_loop(1, lines, own_page, 0)
    for step in range(lines, planes):
        page_from(my_plane ^ step).wait_recv()
        relay(my_plane ^ step).start()
    finish_page(my_plane)

    def other_page(step, carry):
        plane = my_plane ^ (step ^ (step // 2))
        relayed(plane).wait_recv()

        hops = list(range(lines))
        block(*[my_line ^ hop for hop in hops], plane=plane)

        @pl.when(step == planes - 1)
        def _():
            for hop in hops[1:]:
                finish_line(my_line ^ hop)

        finish_page(plane)

        @pl.when(step > 1)
        def _():
            share_page(my_plane ^ ((step - 1) ^ ((step - 1) // 2)))

        return carry

    lax.fori_loop(1, planes, other_page, 0)
    share_page(my_plane ^ ((planes - 1) ^ ((planes - 1) // 2)))

    total = query_acc[my_line]
    for step in range(1, lines):
        part_from(my_line ^ step).wait_recv()
        total += part_in[my_line ^ step].astype(jnp.float32)
    query_grad_ref[...] = total.astype(jnp.bfloat16)

    total = half_page(my_plane)
    for step in range(1, planes):
        share_from(my_plane ^ step).wait_recv()
        total += share_in[my_plane ^ step].astype(jnp.float32)
    page_grad_ref[...] = total.astype(jnp.bfloat16)

    swap(my_plane).wait_send()
    for step in range(1, lines):
        tokens_to(my_line ^ step).wait_send()
        part_to(my_line ^ step).wait_send()
    for step in range(1, planes):
        plane = my_plane ^ step
        page_to(plane).wait_send()
        relay(plane).wait_send()
        swap(plane).wait_send()
        share_to(plane).wait_send()


def dense_shards(queries, pages, pair_page, pair_query, pair_label, hot_pages):
    owners = lax.axis_size("owner")
    replicas = lax.axis_size("replica")
    local_queries, tokens_each, width = queries.shape
    patches = pages.shape[1]
    pairs = pair_query.shape[0]
    rows = local_queries * tokens_each
    flag_rows = 2 * local_queries
    part = patches // replicas
    planes = 4
    lines = owners // planes
    vmem = pl.BlockSpec(memory_space=pltpu.VMEM)
    query_grad, page_grad = pl.pallas_call(
        functools.partial(
            dense_kernel, lines, planes, (local_queries, tokens_each, width, patches)
        ),
        out_shape=(
            jax.ShapeDtypeStruct((rows, width), jnp.bfloat16),
            jax.ShapeDtypeStruct((part, width), jnp.bfloat16),
        ),
        in_specs=[vmem] * 6,
        out_specs=(vmem, vmem),
        scratch_shapes=[
            pltpu.VMEM((lines, rows + flag_rows, width), jnp.bfloat16),
            pltpu.VMEM((planes, replicas, part, width), jnp.bfloat16),
            pltpu.VMEM((planes, width, patches), jnp.float32),
            pltpu.VMEM((lines, rows, width), jnp.float32),
            pltpu.VMEM((planes, replicas, part, width), jnp.float32),
            *[pltpu.VMEM((planes, part, width), jnp.bfloat16)] * 4,
            *[pltpu.VMEM((lines, rows, width), jnp.bfloat16)] * 2,
            *[pltpu.SemaphoreType.DMA((lines,))] * 2,
            *[pltpu.SemaphoreType.DMA((planes,))] * 8,
            *[pltpu.SemaphoreType.DMA((lines,))] * 2,
        ],
        compiler_params=pltpu.CompilerParams(
            collective_id=0, has_side_effects=True, vmem_limit_bytes=24 << 20
        ),
    )(
        queries.reshape(rows, width),
        pages[0],
        pair_page.reshape(1, pairs),
        pair_query.reshape(1, pairs),
        pair_label.reshape(1, pairs),
        hot_pages.reshape(1, hot_pages.shape[0]),
    )
    return query_grad.reshape(queries.shape), page_grad[None]


SHARPNESS = 4.0
SLOPE_SCALE = 0.5
HOT_SHIFT = 2.0


def score_block(token_rows, label_rows, page_rows, offset, shift):
    count = token_rows.shape[0]
    tokens_each = token_rows.shape[1]
    flat_rows = token_rows.reshape(count * tokens_each, token_rows.shape[2])
    logits = SHARPNESS * lax.dot_general(
        flat_rows, page_rows, (((1,), (1,)), ((), ())), preferred_element_type=jnp.float32
    )
    peak = jnp.max(logits, axis=1, keepdims=True)
    expo = jnp.exp(logits - peak)
    totals = jnp.sum(expo, axis=1, keepdims=True)
    log_total = peak + jnp.log(totals)
    score = jnp.sum(log_total.reshape(count, tokens_each), axis=1) / SHARPNESS
    logit = SLOPE_SCALE * score + offset - shift
    slope = SLOPE_SCALE * (jax.nn.sigmoid(logit) - label_rows[:, 0]) * label_rows[:, 1]
    slope_rows = jnp.repeat(slope, tokens_each)[:, None]
    weight = (expo / totals * slope_rows).astype(jnp.bfloat16)
    grads = jnp.dot(weight, page_rows, preferred_element_type=jnp.float32).astype(jnp.bfloat16)
    page_part = lax.dot_general(
        weight, flat_rows, (((0,), (0,)), ((), ())), preferred_element_type=jnp.float32
    )
    return (grads.reshape(token_rows.shape), page_part)


def sparse_shards(queries, pages, pair_page, pair_query, pair_label, hot_pages):
    owners = lax.axis_size("owner")
    owner_place = lax.axis_index("owner")
    local_pairs = pair_page.shape[0]
    local_queries = queries.shape[0]
    tokens_each = queries.shape[1]
    width = queries.shape[2]
    patch_count = pages.shape[1]
    capacity = max(2, 4 * local_pairs // owners)
    slots = owners * capacity
    offset = -SLOPE_SCALE * tokens_each * (math.log(patch_count) / SHARPNESS + SHARPNESS / 2.0)
    targets = pair_page[:, 0]
    owned_hot = (hot_pages == owner_place).astype(jnp.float32)
    target_hot = (targets[:, None] == jnp.arange(owners, dtype=jnp.int32)[None, :]).astype(
        jnp.int32
    )
    earlier = jnp.cumsum(target_hot, axis=0) - target_hot
    rank_within = jnp.sum(earlier * target_hot, axis=1)
    slot_of = targets * capacity + rank_within
    select = (slot_of[None, :] == jnp.arange(slots, dtype=jnp.int32)[:, None]).astype(jnp.bfloat16)
    query_hot = (pair_query[:, None] == jnp.arange(local_queries, dtype=jnp.int32)[None, :]).astype(
        jnp.bfloat16
    )
    pair_tokens = jnp.dot(
        query_hot,
        queries.reshape(local_queries, tokens_each * width),
        preferred_element_type=jnp.float32,
    ).astype(jnp.bfloat16)
    send_tokens = jnp.dot(select, pair_tokens, preferred_element_type=jnp.float32).astype(
        jnp.bfloat16
    )
    pair_flags = jnp.stack(
        [pair_label.astype(jnp.float32), jnp.ones((local_pairs,), jnp.float32)], axis=1
    ).astype(jnp.bfloat16)
    send_flags = jnp.dot(select, pair_flags, preferred_element_type=jnp.float32).astype(
        jnp.bfloat16
    )
    got_tokens, got_flags = (
        lax.all_to_all(
            send_tokens.reshape(owners, capacity * tokens_each * width),
            "owner",
            split_axis=0,
            concat_axis=0,
            tiled=True,
        ),
        lax.all_to_all(
            send_flags.reshape(owners, capacity * 2),
            "owner",
            split_axis=0,
            concat_axis=0,
            tiled=True,
        ),
    )
    slot_tokens = got_tokens.reshape(slots, tokens_each, width)
    slot_flags = got_flags.reshape(slots, 2).astype(jnp.float32)
    page_rows = pages[0]
    own_shift = HOT_SHIFT * jnp.sum(owned_hot)
    block_rows = slots // max(1, slots // 64)
    filled = (slot_flags[:, 1] > 0.5).astype(jnp.int32)
    order = jnp.argsort(1 - filled, stable=True)
    inverse = jnp.argsort(order, stable=True)
    sorted_tokens = slot_tokens[order]
    sorted_flags = slot_flags[order]
    live_blocks = (jnp.sum(filled) + block_rows - 1) // block_rows

    def visit(block_id, carry):
        grad_store, page_acc = carry
        start = (block_id * block_rows).astype(jnp.int32)
        token_rows = lax.dynamic_slice_in_dim(sorted_tokens, start, block_rows, 0)
        label_rows = lax.dynamic_slice_in_dim(sorted_flags, start, block_rows, 0)
        grads, page_part = score_block(token_rows, label_rows, page_rows, offset, own_shift)
        grad_store = lax.dynamic_update_slice_in_dim(grad_store, grads, start, 0)
        return (grad_store, page_acc + page_part)

    sorted_grads, page_terms = lax.fori_loop(
        0,
        live_blocks,
        visit,
        (
            jnp.zeros((slots, tokens_each, width), jnp.bfloat16),
            jnp.zeros((patch_count, width), jnp.float32),
        ),
    )
    slot_grads = sorted_grads[inverse]
    returned = lax.all_to_all(
        slot_grads.reshape(owners, capacity * tokens_each * width),
        "owner",
        split_axis=0,
        concat_axis=0,
        tiled=True,
    )
    pair_grads = lax.dot_general(
        select,
        returned.reshape(slots, tokens_each * width),
        (((0,), (0,)), ((), ())),
        preferred_element_type=jnp.float32,
    )
    summed = lax.dot_general(
        query_hot.astype(jnp.float32),
        pair_grads,
        (((0,), (0,)), ((), ())),
        precision=lax.Precision.HIGHEST,
        preferred_element_type=jnp.float32,
    )
    query_grad = summed.reshape(local_queries, tokens_each, width).astype(jnp.bfloat16)
    page_share = lax.psum_scatter(
        page_terms.astype(jnp.bfloat16), "replica", scatter_dimension=0, tiled=True
    )
    return (query_grad, page_share[None])


def shards(queries, pages, pair_page, pair_query, pair_label, hot_pages):
    owners = lax.axis_size("owner")
    replicas = lax.axis_size("replica")
    local_pairs = pair_query.shape[0]
    local_queries = queries.shape[0]
    capacity = max(2, 4 * local_pairs // owners)
    dense = capacity >= local_queries and owners <= queries.shape[2] and replicas == 2
    dense = dense and owners % 8 == 0 and owners & (owners - 1) == 0
    plan = dense_shards if dense else sparse_shards
    return plan(queries, pages, pair_page, pair_query, pair_label, hot_pages)


def solution(mesh):
    placed = (
        P(("owner", "replica"), None, None),
        P("owner", None, None),
        P(("owner", "replica"), None),
        P(("owner", "replica")),
        P(("owner", "replica")),
        P(),
    )
    return jax.shard_map(
        shards,
        mesh=mesh,
        in_specs=placed,
        out_specs=(P(("owner", "replica"), None, None), P("owner", "replica", None)),
        check_vma=False,
    )
```

profile of v0, /device:TPU:0, one launch (start us, length us, event | category | flops | bytes accessed | tf_op | source)
XLA Modules:
  0.0 33.9 jit_solution(4674206479927973047)
XLA Ops:
  0.6 0.0 copy-start.5
  0.6 0.0 copy-start.2
  0.7 0.0 copy-start.3
  0.7 0.0 copy-start.4
  0.7 0.6 %copy-done.5 = s32[2]{0:T(128)S(1)} copy-done((s32[2]{0:T(128)S(1)}, s32[2]{0:T(128)}, u32[]{:S(2)}) %copy-start.5) | copy-done | bytes 32
  1.3 0.0 copy-done.2
  1.3 0.0 copy-done.3
  1.3 0.0 copy-done.4
  1.3 0.0 copy-start
  1.3 0.9 %copy-done = bf16[1,1024,128]{2,1,0:T(8,128)(2,1)S(1)} copy-done((bf16[1,1024,128]{2,1,0:T(8,128)(2,1)S(1)}, bf16[1,1024,128]{2,1,0:T(8,128)(2,1)}, u32[]{:S(2)}) %copy-start) | copy-done | bytes 262168
  2.3 0.0 copy-start.1
  2.3 0.8 %copy-done.1 = bf16[8,32,128]{2,1,0:T(8,128)(2,1)S(1)} copy-done((bf16[8,32,128]{2,1,0:T(8,128)(2,1)S(1)}, bf16[8,32,128]{2,1,0:T(8,128)(2,1)}, u32[]{:S(2)}) %copy-start.1) | copy-done | bytes 65560
  3.1 29.5 %shard_map.77 = (bf16[256,128]{1,0:T(8,128)(2,1)S(1)}, bf16[512,128]{1,0:T(8,128)(2,1)S(1)}) custom-call(bf16[256,128]{1,0:T(8,128)(2,1)S(1)} %bitcast.10, bf16[1024,128]{1,0:T(8,128)(2,1)S(1)} %bitcast.8, s32[1,64]{1,0:T(1,128)S(1)} %bitcast.12, s32[1,64]{1,0:T(1,128)S(1)} %bitcast.13, s32[1,64]{1,0:T(1,128)S(1)} %bitcast.14, s32[1,2]{1,0:T(1,128)S(1)} %bitcast.15), custom_call_target="tpu_custom_call" | custom-call | tf_op jit(solution)/shard_map/pallas_call | solution.py:317
  32.6 0.6 %copy.10 = bf16[8,32,128]{2,1,0:T(8,128)(2,1)} copy(bf16[8,32,128]{2,1,0:T(8,128)(2,1)S(1)} %bitcast.11) | data formatting | bytes 131072
  33.3 0.7 %copy.11 = bf16[1,512,128]{2,1,0:T(8,128)(2,1)} copy(bf16[1,512,128]{2,1,0:T(8,128)(2,1)S(1)} %bitcast.9) | data formatting | bytes 262144
Async XLA Ops:
  0.6 0.7 %copy-start.5 = (s32[2]{0:T(128)S(1)}, s32[2]{0:T(128)}, u32[]{:S(2)}) copy-start(s32[2]{0:T(128)} %param.11) | copy-start | bytes 28
  0.6 0.7 %copy-start.2 = (s32[64,1]{0,1:T(1,128)S(1)}, s32[64,1]{0,1:T(1,128)}, u32[]{:S(2)}) copy-start(s32[64,1]{0,1:T(1,128)} %param.8) | copy-start | bytes 772
  0.7 0.7 %copy-start.3 = (s32[64]{0:T(128)S(1)}, s32[64]{0:T(128)}, u32[]{:S(2)}) copy-start(s32[64]{0:T(128)} %param.9) | copy-start | bytes 772
  0.7 0.7 %copy-start.4 = (s32[64]{0:T(128)S(1)}, s32[64]{0:T(128)}, u32[]{:S(2)}) copy-start(s32[64]{0:T(128)} %param.10) | copy-start | bytes 772
  1.3 0.9 %copy-start = (bf16[1,1024,128]{2,1,0:T(8,128)(2,1)S(1)}, bf16[1,1024,128]{2,1,0:T(8,128)(2,1)}, u32[]{:S(2)}) copy-start(bf16[1,1024,128]{2,1,0:T(8,128)(2,1)} %param.7) | copy-start | bytes 786436
  2.3 0.8 %copy-start.1 = (bf16[8,32,128]{2,1,0:T(8,128)(2,1)S(1)}, bf16[8,32,128]{2,1,0:T(8,128)(2,1)}, u32[]{:S(2)}) copy-start(bf16[8,32,128]{2,1,0:T(8,128)(2,1)} %param.6) | copy-start | bytes 196612
where the time goes:
time: 34.1 us; the launch traced here: 33.9 us
  Pallas kernels  29.5 us (87%)
  local copies, waits for them, and re-layouts  3.75 us (11%)
  between operations  0.68 us (2%)
    pallas_call x1, Pallas kernels, dense_shards(): pl.pallas_call(functools.partial(dense_kernel, lines, planes, (local_quer...  29.5 us
    unnamed x14, local copies, waits for them, and re-layouts  3.75 us

commit v1 on v0

--- a/solution.py
+++ b/solution.py
@@ -11,18 +11,54 @@
 MESH = pl.DeviceIdType.MESH
 
 
+ORDER = range(4)
+
+def plan():
+    return (
+        ("tokens", 1),
+        ("block", (1, 0)),
+        ("page", 1),
+        ("page", 2),
+        ("page", 3),
+        ("tokens", 3),
+        ("tokens", 2),
+        ("block", (3, 0), (2, 0)),
+        ("finish", 0),
+        ("relayed", 3),
+        ("block", (0, 3), (1, 3), (3, 3), (2, 3)),
+        ("finish", 3),
+        ("relayed", 1),
+        ("block", (0, 1), (1, 1), (3, 1), (2, 1)),
+        ("finish", 1),
+        ("share", 3),
+        ("relayed", 2),
+        ("block", (2, 2), (3, 2)),
+        ("line", 2),
+        ("line", 3),
+        ("share", 1),
+        ("block", (1, 2), (0, 2)),
+        ("line", 1),
+        ("finish", 2),
+        ("share", 2),
+    )
+
+
 def dense_kernel(
     lines,
     planes,
     shapes,
     query_ref,
     page_ref,
+    pair_page_hbm,
+    pair_query_hbm,
+    pair_label_hbm,
+    hot_hbm,
+    query_grad_ref,
+    page_grad_ref,
     pair_page_ref,
     pair_query_ref,
     pair_label_ref,
     hot_ref,
-    query_grad_ref,
-    page_grad_ref,
     held,
     paged,
     page_acc,
@@ -34,8 +70,11 @@
     share_in,
     part_out,
     part_in,
+    load_sem,
     line_sem,
     line_in_sem,
+    flag_sem,
+    flag_in_sem,
     plane_sem,
     plane_in_sem,
     relay_sem,
@@ -50,11 +89,21 @@
     local_queries, tokens_each, width, patches = shapes
     rows = local_queries * tokens_each
     flag_rows = held.shape[1] - rows
-    part = patches // 2
     me = lax.axis_index("owner")
     core = lax.axis_index("replica")
-
     my_line, my_plane = me // planes, me % planes
+
+    def load(src, dst, place):
+        return pltpu.make_async_copy(src, dst, load_sem.at[place])
+
+    loads = [
+        load(pair_page_hbm, pair_page_ref, 0),
+        load(pair_query_hbm, pair_query_ref, 1),
+        load(pair_label_hbm, pair_label_ref, 2),
+        load(hot_hbm, hot_ref, 3),
+        load(query_ref, held.at[my_line, pl.ds(0, rows), :], 4),
+        load(page_ref, paged.at[my_plane], 5),
+    ]
 
     barrier = pltpu.get_barrier_semaphore()
 
@@ -66,9 +115,96 @@
     for step in range(1, planes):
         greet(my_line * planes + (my_plane ^ step))
     pl.semaphore_signal(barrier, inc=1, device_id={"replica": 1 - core}, device_id_type=MESH)
+    for copy in loads:
+        copy.start()
+
+    def remote(src, dst, sent, received, device):
+        return pltpu.make_async_remote_copy(
+            src_ref=src,
+            dst_ref=dst,
+            send_sem=sent,
+            recv_sem=received,
+            device_id=device,
+            device_id_type=MESH,
+        )
+
+    def to_line(line):
+        return {"owner": line * planes + my_plane}
+
+    def to_plane(plane):
+        return {"owner": my_line * planes + plane}
+
+    twin = {"replica": 1 - core}
+
+    def tokens_to(line):
+        dst = held.at[my_line, pl.ds(0, rows), :]
+        return remote(query_ref, dst, line_sem.at[line], line_in_sem.at[my_line], to_line(line))
+
+    def tokens_from(line):
+        slot = held.at[line, pl.ds(0, rows), :]
+        return remote(slot, slot, line_sem.at[line], line_in_sem.at[line], to_line(line))
+
+    def flags_to(line):
+        slot = held.at[my_line, pl.ds(rows, flag_rows), :]
+        return remote(slot, slot, flag_sem.at[line], flag_in_sem.at[my_line], to_line(line))
+
+    def flags_from(line):
+        slot = held.at[line, pl.ds(rows, flag_rows), :]
+        return remote(slot, slot, flag_sem.at[line], flag_in_sem.at[line], to_line(line))
+
+    def page_to(plane):
+        src, dst = page_ref.at[core], paged.at[my_plane, core]
+        return remote(src, dst, plane_sem.at[plane], plane_in_sem.at[my_plane], to_plane(plane))
+
+    def page_from(plane):
+        slot = paged.at[plane, core]
+        return remote(slot, slot, plane_sem.at[plane], plane_in_sem.at[plane], to_plane(plane))
+
+    def relay(plane):
+        slot = paged.at[plane, core]
+        return remote(slot, slot, relay_sem.at[plane], relay_in_sem.at[plane], twin)
+
+    def relayed(plane):
+        slot = paged.at[plane, 1 - core]
+        return remote(slot, slot, relay_sem.at[plane], relay_in_sem.at[plane], twin)
+
+    def swap(plane):
+        return remote(
+            swap_out.at[plane], swap_in.at[plane], swap_sem.at[plane], swap_in_sem.at[plane], twin
+        )
+
+    def share_to(plane):
+        dst = share_in.at[my_plane]
+        sent, received = share_sem.at[plane], share_in_sem.at[my_plane]
+        return remote(share_out.at[plane], dst, sent, received, to_plane(plane))
+
+    def share_from(plane):
+        dst = share_in.at[plane]
+        sent, received = share_sem.at[plane], share_in_sem.at[plane]
+        return remote(share_out.at[plane], dst, sent, received, to_plane(plane))
+
+    def part_to(line):
+        dst = part_in.at[my_line]
+        sent, received = part_sem.at[line], part_in_sem.at[my_line]
+        return remote(part_out.at[line], dst, sent, received, to_line(line))
+
+    def part_from(line):
+        dst = part_in.at[line]
+        sent, received = part_sem.at[line], part_in_sem.at[line]
+        return remote(part_out.at[line], dst, sent, received, to_line(line))
+
+    pl.semaphore_wait(barrier, lines + planes - 1)
+    page_to(my_plane ^ 1).start()
+    page_to(my_plane ^ 2).start()
+    tokens_to(my_line ^ 1).start()
+    tokens_to(my_line ^ 3).start()
+    tokens_to(my_line ^ 2).start()
+    page_to(my_plane ^ 3).start()
 
     pairs = pair_page_ref.shape[1]
     lanes = held.shape[2]
+    for copy in loads[:4]:
+        copy.wait()
     page_hot = (
         lax.broadcasted_iota(jnp.int32, (lanes, pairs), 0) == pair_page_ref[...]
     ).astype(jnp.float32)
@@ -79,8 +215,9 @@
     flags = lax.dot_general(
         stacked, page_hot, (((1,), (1,)), ((), ())), preferred_element_type=jnp.float32
     )
-    held[my_line, pl.ds(0, rows), :] = query_ref[...]
     held[my_line, pl.ds(rows, flag_rows), :] = flags.astype(jnp.bfloat16)
+    for step in range(1, lines):
+        flags_to(my_line ^ step).start()
 
     offset = -0.5 * tokens_each * (math.log(patches) / 4.0 + 2.0)
 
@@ -89,16 +226,11 @@
     count_pick = (flag_row == row_query).astype(jnp.bfloat16)
     label_pick = (flag_row == row_query + local_queries).astype(jnp.bfloat16)
     lane = lax.broadcasted_iota(jnp.int32, (1, lanes), 1)
-
-    paged[my_plane] = page_ref[...].reshape(paged.shape[1:])
-    page_acc[...] = jnp.zeros_like(page_acc)
-    query_acc[...] = jnp.zeros_like(query_acc)
     scale = 4.0 * math.log2(math.e)
 
     def logits(line, plane):
-        tokens = held[line, pl.ds(0, rows), :]
         return lax.dot_general(
-            tokens,
+            held[line, pl.ds(0, rows), :],
             paged[plane].reshape(patches, width),
             (((1,), (1,)), ((), ())),
             preferred_element_type=jnp.float32,
@@ -129,154 +261,76 @@
         slope = 0.5 * (counts * jax.nn.sigmoid(logit) - labels)
         return (expo * (slope / totals)).astype(jnp.bfloat16)
 
-    def gradients(weight, line, plane):
+    started_lines, started_pages = set(), set()
+
+    def gradients(weight, line, plane, first_line, first_page):
         tokens = held[line, pl.ds(0, rows), :]
-        query_acc[line] += jnp.dot(
+        by_query = jnp.dot(
             weight, paged[plane].reshape(patches, width), preferred_element_type=jnp.float32
         )
-        page_acc[plane] += lax.dot_general(
+        by_page = lax.dot_general(
             tokens, weight, (((0,), (0,)), ((), ())), preferred_element_type=jnp.float32
         )
-
-    def block(*lines_of, plane):
-        dots = [logits(line, plane) for line in lines_of]
-        for line, dot in zip(lines_of, dots):
-            gradients(weights(dot, line, plane), line, plane)
-
-    block(my_line, plane=my_plane)
-    pl.semaphore_wait(barrier, lines + planes - 1)
-
-    def remote(src, dst, sent, received, device):
-        return pltpu.make_async_remote_copy(
-            src_ref=src,
-            dst_ref=dst,
-            send_sem=sent,
-            recv_sem=received,
-            device_id=device,
-            device_id_type=MESH,
-        )
-
-    def to_line(line):
-        return {"owner": line * planes + my_plane}
-
-    def to_plane(plane):
-        return {"owner": my_line * planes + plane}
-
-    twin = {"replica": 1 - core}
-
-    def tokens_to(line):
-        slot = held.at[my_line]
-        return remote(slot, slot, line_sem.at[line], line_in_sem.at[my_line], to_line(line))
-
-    def tokens_from(line):
-        slot = held.at[line]
-        return remote(slot, slot, line_sem.at[line], line_in_sem.at[line], to_line(line))
-
-    def page_to(plane):
-        src = page_ref.at[pl.ds(core * part, part), :]
-        dst = paged.at[my_plane, core]
-        return remote(src, dst, plane_sem.at[plane], plane_in_sem.at[my_plane], to_plane(plane))
-
-    def page_from(plane):
-        slot = paged.at[plane, core]
-        return remote(slot, slot, plane_sem.at[plane], plane_in_sem.at[plane], to_plane(plane))
-
-    def relay(plane):
-        slot = paged.at[plane, core]
-        return remote(slot, slot, relay_sem.at[plane], relay_in_sem.at[plane], twin)
-
-    def relayed(plane):
-        slot = paged.at[plane, 1 - core]
-        return remote(slot, slot, relay_sem.at[plane], relay_in_sem.at[plane], twin)
-
-    def swap(plane):
-        return remote(
-            swap_out.at[plane], swap_in.at[plane], swap_sem.at[plane], swap_in_sem.at[plane], twin
-        )
-
-    def share_to(plane):
-        dst = share_in.at[my_plane]
-        sent, received = share_sem.at[plane], share_in_sem.at[my_plane]
-        return remote(share_out.at[plane], dst, sent, received, to_plane(plane))
-
-    def share_from(plane):
-        dst = share_in.at[plane]
-        sent, received = share_sem.at[plane], share_in_sem.at[plane]
-        return remote(share_out.at[plane], dst, sent, received, to_plane(plane))
-
-    def part_to(line):
-        dst = part_in.at[my_line]
-        sent, received = part_sem.at[line], part_in_sem.at[my_line]
-        return remote(part_out.at[line], dst, sent, received, to_line(line))
-
-    def part_from(line):
-        dst = part_in.at[line]
-        sent, received = part_sem.at[line], part_in_sem.at[line]
-        return remote(part_out.at[line], dst, sent, received, to_line(line))
-
-    for step in range(1, max(lines, planes)):
-        if step < planes:
-            page_to(my_plane ^ step).start()
-        if step < lines:
-            tokens_to(my_line ^ step).start()
-
-    def finish_line(line):
-        part_out[line] = query_acc[line].astype(jnp.bfloat16)
-        part_to(line).start()
-
-    def finish_page(plane):
-        page_rows[plane] = page_acc[plane].T.reshape(page_rows.shape[1:])
-        swap_out[plane] = page_rows[plane, 1 - core].astype(jnp.bfloat16)
-        swap(plane).start()
+        query_acc[line] = by_query if first_line else query_acc[line] + by_query
+        page_acc[plane] = by_page if first_page else page_acc[plane] + by_page
+
+    def block(*places):
+        spots = [(my_line ^ hop, my_plane ^ jump) for hop, jump in places]
+        dots = [logits(*spot) for spot in spots]
+        for spot, dot, (hop, jump) in zip(spots, dots, places):
+            fresh = hop not in started_lines, jump not in started_pages
+            started_lines.add(hop)
+            started_pages.add(jump)
+            gradients(weights(dot, *spot), *spot, *fresh)
 
     def half_page(plane):
         swap(plane).wait_recv()
         return page_rows[plane, core] + swap_in[plane].astype(jnp.float32)
 
-    def share_page(plane):
-        share_out[plane] = half_page(plane).astype(jnp.bfloat16)
-        share_to(plane).start()
-
-    def own_page(step, carry):
-        line = my_line ^ step
-        tokens_from(line).wait_recv()
-        block(line, plane=my_plane)
-
-        @pl.when(step < planes)
-        def _():
-            page_from(my_plane ^ step).wait_recv()
-            relay(my_plane ^ step).start()
-
-        return carry
-
-    lax.fori_loop(1, lines, own_page, 0)
-    for step in range(lines, planes):
-        page_from(my_plane ^ step).wait_recv()
-        relay(my_plane ^ step).start()
-    finish_page(my_plane)
-
-    def other_page(step, carry):
-        plane = my_plane ^ (step ^ (step // 2))
-        relayed(plane).wait_recv()
-
-        hops = list(range(lines))
-        block(*[my_line ^ hop for hop in hops], plane=plane)
-
-        @pl.when(step == planes - 1)
-        def _():
-            for hop in hops[1:]:
-                finish_line(my_line ^ hop)
-
-        finish_page(plane)
-
-        @pl.when(step > 1)
-        def _():
-            share_page(my_plane ^ ((step - 1) ^ ((step - 1) // 2)))
-
-        return carry
-
-    lax.fori_loop(1, planes, other_page, 0)
-    share_page(my_plane ^ ((planes - 1) ^ ((planes - 1) // 2)))
+    def act(kind, *what):
+        if kind == "block":
+            block(*what)
+            return
+        offset_by = what[0]
+        line, plane = my_line ^ offset_by, my_plane ^ offset_by
+        if kind == "tokens":
+            tokens_from(line).wait_recv()
+            flags_from(line).wait_recv()
+        elif kind == "send_tokens":
+            tokens_to(line).start()
+        elif kind == "sent_tokens":
+            tokens_to(line).wait_send()
+        elif kind == "send_page":
+            page_to(plane).start()
+        elif kind == "sent_page":
+            page_to(plane).wait_send()
+        elif kind == "page":
+            page_from(plane).wait_recv()
+            relay(plane).start()
+        elif kind == "relayed":
+            relayed(plane).wait_recv()
+        elif kind == "line":
+            part_out[line] = query_acc[line].astype(jnp.bfloat16)
+            part_to(line).start()
+        elif kind == "finish":
+            page_rows[plane] = page_acc[plane].T.reshape(page_rows.shape[1:])
+            swap_out[plane] = page_rows[plane, 1 - core].astype(jnp.bfloat16)
+            swap(plane).start()
+        elif kind == "share":
+            share_out[plane] = half_page(plane).astype(jnp.bfloat16)
+            share_to(plane).start()
+
+    loads[4].wait()
+    loads[5].wait()
+    block((0, 0))
+    for step in plan():
+        act(*step)
+
+    total = half_page(my_plane)
+    for step in range(1, planes):
+        share_from(my_plane ^ step).wait_recv()
+        total += share_in[my_plane ^ step].astype(jnp.float32)
+    page_grad_ref[...] = total.astype(jnp.bfloat16)
 
     total = query_acc[my_line]
     for step in range(1, lines):
@@ -284,22 +338,21 @@
         total += part_in[my_line ^ step].astype(jnp.float32)
     query_grad_ref[...] = total.astype(jnp.bfloat16)
 
-    total = half_page(my_plane)
-    for step in range(1, planes):
-        share_from(my_plane ^ step).wait_recv()
-        total += share_in[my_plane ^ step].astype(jnp.float32)
-    page_grad_ref[...] = total.astype(jnp.bfloat16)
-
     swap(my_plane).wait_send()
     for step in range(1, lines):
-        tokens_to(my_line ^ step).wait_send()
+        flags_to(my_line ^ step).wait_send()
         part_to(my_line ^ step).wait_send()
     for step in range(1, planes):
         plane = my_plane ^ step
-        page_to(plane).wait_send()
         relay(plane).wait_send()
         swap(plane).wait_send()
         share_to(plane).wait_send()
+    tokens_to(my_line ^ 1).wait_send()
+    tokens_to(my_line ^ 2).wait_send()
+    tokens_to(my_line ^ 3).wait_send()
+    page_to(my_plane ^ 1).wait_send()
+    page_to(my_plane ^ 2).wait_send()
+    page_to(my_plane ^ 3).wait_send()
 
 
 def dense_shards(queries, pages, pair_page, pair_query, pair_label, hot_pages):
@@ -311,9 +364,10 @@
     rows = local_queries * tokens_each
     flag_rows = 2 * local_queries
     part = patches // replicas
-    planes = 4
+    planes = math.isqrt(owners)
     lines = owners // planes
     vmem = pl.BlockSpec(memory_space=pltpu.VMEM)
+    hbm = pl.BlockSpec(memory_space=pltpu.HBM)
     query_grad, page_grad = pl.pallas_call(
         functools.partial(
             dense_kernel, lines, planes, (local_queries, tokens_each, width, patches)
@@ -322,9 +376,11 @@
             jax.ShapeDtypeStruct((rows, width), jnp.bfloat16),
             jax.ShapeDtypeStruct((part, width), jnp.bfloat16),
         ),
-        in_specs=[vmem] * 6,
+        in_specs=[hbm] * 6,
         out_specs=(vmem, vmem),
         scratch_shapes=[
+            *[pltpu.VMEM((1, pairs), jnp.int32)] * 3,
+            pltpu.VMEM((1, hot_pages.shape[0]), jnp.int32),
             pltpu.VMEM((lines, rows + flag_rows, width), jnp.bfloat16),
             pltpu.VMEM((planes, replicas, part, width), jnp.bfloat16),
             pltpu.VMEM((planes, width, patches), jnp.float32),
@@ -332,7 +388,8 @@
             pltpu.VMEM((planes, replicas, part, width), jnp.float32),
             *[pltpu.VMEM((planes, part, width), jnp.bfloat16)] * 4,
             *[pltpu.VMEM((lines, rows, width), jnp.bfloat16)] * 2,
-            *[pltpu.SemaphoreType.DMA((lines,))] * 2,
+            pltpu.SemaphoreType.DMA((6,)),
+            *[pltpu.SemaphoreType.DMA((lines,))] * 4,
             *[pltpu.SemaphoreType.DMA((planes,))] * 8,
             *[pltpu.SemaphoreType.DMA((lines,))] * 2,
         ],
@@ -340,12 +397,17 @@
             collective_id=0, has_side_effects=True, vmem_limit_bytes=24 << 20
         ),
     )(
-        queries.reshape(rows, width),
-        pages[0],
-        pair_page.reshape(1, pairs),
-        pair_query.reshape(1, pairs),
-        pair_label.reshape(1, pairs),
-        hot_pages.reshape(1, hot_pages.shape[0]),
+        *[
+            pltpu.with_memory_space_constraint(operand, pltpu.HBM)
+            for operand in (
+                queries.reshape(rows, width),
+                pages[0].reshape(replicas, part, width),
+                pair_page.reshape(1, pairs),
+                pair_query.reshape(1, pairs),
+                pair_label.reshape(1, pairs),
+                hot_pages.reshape(1, hot_pages.shape[0]),
+            )
+        ]
     )
     return query_grad.reshape(queries.shape), page_grad[None]
 
@@ -496,7 +558,7 @@
     local_queries = queries.shape[0]
     capacity = max(2, 4 * local_pairs // owners)
     dense = capacity >= local_queries and owners <= queries.shape[2] and replicas == 2
-    dense = dense and owners % 8 == 0 and owners & (owners - 1) == 0
+    dense = dense and owners == len(ORDER) ** 2
     plan = dense_shards if dense else sparse_shards
     return plan(queries, pages, pair_page, pair_query, pair_label, hot_pages)
 

time: 34.1 us -> 32.2 us (0.944)
  local copies, waits for them, and re-layouts: 3.75 us -> 1.29 us
  Pallas kernels: 29.5 us -> 30.1 us
    unnamed x14 -> x2, local copies, waits for them, and re-layouts: 3.75 us -> 1.29 us
    pallas_call x1, Pallas kernels: 29.5 us -> 30.1 us  [dense_shards(): pl.pallas_call(functools.partial(dense_kernel, lines, planes, (local_quer...]
where the time goes in v1:
time: 32.2 us; the launch traced here: 32.1 us
  Pallas kernels  30.1 us (93%)
  local copies, waits for them, and re-layouts  1.29 us (4%)
  between operations  0.64 us (2%)
    pallas_call x1, Pallas kernels, dense_shards(): pl.pallas_call(functools.partial(dense_kernel, lines, planes, (local_quer...  30.1 us
    unnamed x2, local copies, waits for them, and re-layouts  1.29 us

profile of v1, /device:TPU:0, one launch (start us, length us, event | category | flops | bytes accessed | tf_op | source)
XLA Modules:
  0.0 32.1 jit_solution(12698589728535281667)
XLA Ops:
  0.6 30.1 %shard_map.77 = (bf16[256,128]{1,0:T(8,128)(2,1)S(1)}, bf16[512,128]{1,0:T(8,128)(2,1)S(1)}) custom-call(bf16[256,128]{1,0:T(8,128)(2,1)} %bitcast.11, bf16[2,512,128]{2,1,0:T(8,128)(2,1)} %bitcast.10, s32[1,64]{1,0:T(1,128)} %bitcast.12, s32[1,64]{1,0:T(1,128)} %bitcast.13, s32[1,64]{1,0:T(1,128)} %bitcast.14, s32[1,2]{1,0:T(1,128)} %bitcast.15), custom_call_target="tpu_custom_call" | custom-call | tf_op jit(solution)/shard_map/pallas_call | solution.py:371
  30.8 0.6 %copy.10 = bf16[8,32,128]{2,1,0:T(8,128)(2,1)} copy(bf16[8,32,128]{2,1,0:T(8,128)(2,1)S(1)} %bitcast.9) | data formatting | bytes 131072
  31.4 0.7 %copy.11 = bf16[1,512,128]{2,1,0:T(8,128)(2,1)} copy(bf16[1,512,128]{2,1,0:T(8,128)(2,1)S(1)} %bitcast.8) | data formatting | bytes 262144

commit v2 on v1

--- a/solution.py
+++ b/solution.py
@@ -18,28 +18,29 @@
         ("tokens", 1),
         ("block", (1, 0)),
         ("page", 1),
-        ("page", 2),
+        ("send_page", 3),
+        ("send_tokens", 2),
+        ("block", (0, 1), (1, 1)),
+        ("tokens", 3),
+        ("block", (3, 1), (3, 0)),
+        ("relayed", 2),
+        ("block", (0, 2), (1, 2), (3, 2)),
         ("page", 3),
-        ("tokens", 3),
         ("tokens", 2),
-        ("block", (3, 0), (2, 0)),
-        ("finish", 0),
+        ("block", (2, 1), (2, 2)),
+        ("finish", 1),
+        ("finish", 2),
         ("relayed", 3),
-        ("block", (0, 3), (1, 3), (3, 3), (2, 3)),
-        ("finish", 3),
-        ("relayed", 1),
-        ("block", (0, 1), (1, 1), (3, 1), (2, 1)),
-        ("finish", 1),
-        ("share", 3),
-        ("relayed", 2),
-        ("block", (2, 2), (3, 2)),
-        ("line", 2),
+        ("block", (3, 3), (2, 3)),
         ("line", 3),
         ("share", 1),
-        ("block", (1, 2), (0, 2)),
+        ("share", 2),
+        ("block", (2, 0), (1, 3), (0, 3)),
+        ("finish", 3),
+        ("line", 2),
         ("line", 1),
-        ("finish", 2),
-        ("share", 2),
+        ("finish", 0),
+        ("share", 3),
     )
 
 
@@ -63,7 +64,6 @@
     paged,
     page_acc,
     query_acc,
-    page_rows,
     swap_out,
     swap_in,
     share_out,
@@ -89,6 +89,7 @@
     local_queries, tokens_each, width, patches = shapes
     rows = local_queries * tokens_each
     flag_rows = held.shape[1] - rows
+    part = page_acc.shape[3]
     me = lax.axis_index("owner")
     core = lax.axis_index("replica")
     my_line, my_plane = me // planes, me % planes
@@ -115,6 +116,8 @@
     for step in range(1, planes):
         greet(my_line * planes + (my_plane ^ step))
     pl.semaphore_signal(barrier, inc=1, device_id={"replica": 1 - core}, device_id_type=MESH)
+    across = {"owner": my_line * planes + (my_plane ^ (1 + core)), "replica": 1 - core}
+    pl.semaphore_signal(barrier, inc=1, device_id=across, device_id_type=MESH)
     for copy in loads:
         copy.start()
 
@@ -137,8 +140,8 @@
     twin = {"replica": 1 - core}
 
     def tokens_to(line):
-        dst = held.at[my_line, pl.ds(0, rows), :]
-        return remote(query_ref, dst, line_sem.at[line], line_in_sem.at[my_line], to_line(line))
+        slot = held.at[my_line, pl.ds(0, rows), :]
+        return remote(slot, slot, line_sem.at[line], line_in_sem.at[my_line], to_line(line))
 
     def tokens_from(line):
         slot = held.at[line, pl.ds(0, rows), :]
@@ -152,20 +155,33 @@
         slot = held.at[line, pl.ds(rows, flag_rows), :]
         return remote(slot, slot, flag_sem.at[line], flag_in_sem.at[line], to_line(line))
 
-    def page_to(plane):
-        src, dst = page_ref.at[core], paged.at[my_plane, core]
-        return remote(src, dst, plane_sem.at[plane], plane_in_sem.at[my_plane], to_plane(plane))
-
-    def page_from(plane):
-        slot = paged.at[plane, core]
-        return remote(slot, slot, plane_sem.at[plane], plane_in_sem.at[plane], to_plane(plane))
-
-    def relay(plane):
-        slot = paged.at[plane, core]
+    def turn(jump):
+        return my_plane ^ (0, 1 + core, 2 - core, 3)[jump]
+
+    def page_to(jump):
+        slot = paged.at[my_plane, core]
+        plane = my_plane ^ jump
+        device = {"owner": my_line * planes + plane, "replica": jump - 1}
+        return remote(slot, slot, plane_sem.at[plane], plane_in_sem.at[my_plane, core], device)
+
+    def page_on():
+        slot = paged.at[turn(1), core]
+        sent, received = plane_sem.at[turn(3)], plane_in_sem.at[turn(1), core]
+        return remote(slot, slot, sent, received, to_plane(turn(2)))
+
+    def page_from(plane, side):
+        slot = paged.at[plane, side]
+        sent, received = plane_sem.at[plane], plane_in_sem.at[plane, side]
+        return remote(slot, slot, sent, received, to_plane(plane))
+
+    def relay(jump):
+        plane = turn(jump)
+        slot = paged.at[plane] if jump < 3 else paged.at[plane, core]
         return remote(slot, slot, relay_sem.at[plane], relay_in_sem.at[plane], twin)
 
-    def relayed(plane):
-        slot = paged.at[plane, 1 - core]
+    def relayed(jump):
+        plane = turn(jump)
+        slot = paged.at[plane] if jump < 3 else paged.at[plane, 1 - core]
         return remote(slot, slot, relay_sem.at[plane], relay_in_sem.at[plane], twin)
 
     def swap(plane):
@@ -193,13 +209,13 @@
         sent, received = part_sem.at[line], part_in_sem.at[line]
         return remote(part_out.at[line], dst, sent, received, to_line(line))
 
-    pl.semaphore_wait(barrier, lines + planes - 1)
-    page_to(my_plane ^ 1).start()
-    page_to(my_plane ^ 2).start()
+    loads[4].wait()
+    loads[5].wait()
+    pl.semaphore_wait(barrier, lines + planes)
+    page_to(1).start()
+    page_to(2).start()
     tokens_to(my_line ^ 1).start()
     tokens_to(my_line ^ 3).start()
-    tokens_to(my_line ^ 2).start()
-    page_to(my_plane ^ 3).start()
 
     pairs = pair_page_ref.shape[1]
     lanes = held.shape[2]
@@ -272,10 +288,12 @@
             tokens, weight, (((0,), (0,)), ((), ())), preferred_element_type=jnp.float32
         )
         query_acc[line] = by_query if first_line else query_acc[line] + by_query
-        page_acc[plane] = by_page if first_page else page_acc[plane] + by_page
+        for side in range(page_acc.shape[1]):
+            terms = by_page[:, side * part : (side + 1) * part]
+            page_acc[plane, side] = terms if first_page else page_acc[plane, side] + terms
 
     def block(*places):
-        spots = [(my_line ^ hop, my_plane ^ jump) for hop, jump in places]
+        spots = [(my_line ^ hop, turn(jump)) for hop, jump in places]
         dots = [logits(*spot) for spot in spots]
         for spot, dot, (hop, jump) in zip(spots, dots, places):
             fresh = hop not in started_lines, jump not in started_pages
@@ -285,14 +303,14 @@
 
     def half_page(plane):
         swap(plane).wait_recv()
-        return page_rows[plane, core] + swap_in[plane].astype(jnp.float32)
+        return page_acc[plane, core] + swap_in[plane].astype(jnp.float32)
 
     def act(kind, *what):
         if kind == "block":
             block(*what)
             return
         offset_by = what[0]
-        line, plane = my_line ^ offset_by, my_plane ^ offset_by
+        line, plane = my_line ^ offset_by, turn(offset_by)
         if kind == "tokens":
             tokens_from(line).wait_recv()
             flags_from(line).wait_recv()
@@ -301,42 +319,41 @@
         elif kind == "sent_tokens":
             tokens_to(line).wait_send()
         elif kind == "send_page":
-            page_to(plane).start()
+            page_on().start()
         elif kind == "sent_page":
             page_to(plane).wait_send()
         elif kind == "page":
-            page_from(plane).wait_recv()
-            relay(plane).start()
+            if offset_by < 3:
+                page_from(plane, 1 - core).wait_recv()
+            page_from(plane, core).wait_recv()
+            relay(offset_by).start()
         elif kind == "relayed":
-            relayed(plane).wait_recv()
+            relayed(offset_by).wait_recv()
         elif kind == "line":
             part_out[line] = query_acc[line].astype(jnp.bfloat16)
             part_to(line).start()
         elif kind == "finish":
-            page_rows[plane] = page_acc[plane].T.reshape(page_rows.shape[1:])
-            swap_out[plane] = page_rows[plane, 1 - core].astype(jnp.bfloat16)
+            swap_out[plane] = page_acc[plane, 1 - core].astype(jnp.bfloat16)
             swap(plane).start()
         elif kind == "share":
             share_out[plane] = half_page(plane).astype(jnp.bfloat16)
             share_to(plane).start()
 
-    loads[4].wait()
-    loads[5].wait()
     block((0, 0))
     for step in plan():
         act(*step)
-
-    total = half_page(my_plane)
-    for step in range(1, planes):
-        share_from(my_plane ^ step).wait_recv()
-        total += share_in[my_plane ^ step].astype(jnp.float32)
-    page_grad_ref[...] = total.astype(jnp.bfloat16)
 
     total = query_acc[my_line]
     for step in range(1, lines):
         part_from(my_line ^ step).wait_recv()
         total += part_in[my_line ^ step].astype(jnp.float32)
     query_grad_ref[...] = total.astype(jnp.bfloat16)
+
+    total = half_page(my_plane)
+    for step in range(1, planes):
+        share_from(my_plane ^ step).wait_recv()
+        total += share_in[my_plane ^ step].astype(jnp.float32)
+    page_grad_ref[...] = total.T.astype(jnp.bfloat16)
 
     swap(my_plane).wait_send()
     for step in range(1, lines):
@@ -344,15 +361,27 @@
         part_to(my_line ^ step).wait_send()
     for step in range(1, planes):
         plane = my_plane ^ step
-        relay(plane).wait_send()
         swap(plane).wait_send()
         share_to(plane).wait_send()
+    relay(1).wait_send()
+    relay(3).wait_send()
     tokens_to(my_line ^ 1).wait_send()
     tokens_to(my_line ^ 2).wait_send()
     tokens_to(my_line ^ 3).wait_send()
-    page_to(my_plane ^ 1).wait_send()
-    page_to(my_plane ^ 2).wait_send()
-    page_to(my_plane ^ 3).wait_send()
+    page_to(1).wait_send()
+    page_to(2).wait_send()
+    page_on().wait_send()
+
+
+def store_kernel(query_ref, page_ref, query_out, page_out, sems):
+    copies = [
+        pltpu.make_async_copy(query_ref, query_out, sems.at[0]),
+        pltpu.make_async_copy(page_ref, page_out, sems.at[1]),
+    ]
+    for copy in copies:
+        copy.start()
+    for copy in copies:
+        copy.wait()
 
 
 def dense_shards(queries, pages, pair_page, pair_query, pair_label, hot_pages):
@@ -383,14 +412,15 @@
             pltpu.VMEM((1, hot_pages.shape[0]), jnp.int32),
             pltpu.VMEM((lines, rows + flag_rows, width), jnp.bfloat16),
             pltpu.VMEM((planes, replicas, part, width), jnp.bfloat16),
-            pltpu.VMEM((planes, width, patches), jnp.float32),
+            pltpu.VMEM((planes, replicas, width, part), jnp.float32),
             pltpu.VMEM((lines, rows, width), jnp.float32),
-            pltpu.VMEM((planes, replicas, part, width), jnp.float32),
-            *[pltpu.VMEM((planes, part, width), jnp.bfloat16)] * 4,
+            *[pltpu.VMEM((planes, width, part), jnp.bfloat16)] * 4,
             *[pltpu.VMEM((lines, rows, width), jnp.bfloat16)] * 2,
             pltpu.SemaphoreType.DMA((6,)),
             *[pltpu.SemaphoreType.DMA((lines,))] * 4,
-            *[pltpu.SemaphoreType.DMA((planes,))] * 8,
+            pltpu.SemaphoreType.DMA((planes,)),
+            pltpu.SemaphoreType.DMA((planes, replicas)),
+            *[pltpu.SemaphoreType.DMA((planes,))] * 6,
             *[pltpu.SemaphoreType.DMA((lines,))] * 2,
         ],
         compiler_params=pltpu.CompilerParams(
@@ -409,6 +439,17 @@
             )
         ]
     )
+    query_grad, page_grad = pl.pallas_call(
+        store_kernel,
+        out_shape=(
+            jax.ShapeDtypeStruct(query_grad.shape, query_grad.dtype),
+            jax.ShapeDtypeStruct(page_grad.shape, page_grad.dtype),
+        ),
+        in_specs=[vmem, vmem],
+        out_specs=(hbm, hbm),
+        scratch_shapes=[pltpu.SemaphoreType.DMA((2,))],
+        compiler_params=pltpu.CompilerParams(vmem_limit_bytes=1 << 20),
+    )(query_grad, page_grad)
     return query_grad.reshape(queries.shape), page_grad[None]
 
 

time: 32.2 us -> 28.8 us (0.89)
  Pallas kernels: 30.1 us -> 28 us
  local copies, waits for them, and re-layouts: 1.29 us -> 0 us
    pallas_call x1, Pallas kernels: 30.1 us -> 27.3 us  [dense_shards(): pl.pallas_call(functools.partial(dense_kernel, lines, planes, (local_quer...]
    unnamed x2 -> x0, local copies, waits for them, and re-layouts: 1.29 us -> none
    pallas_call x0 -> x1, Pallas kernels: none -> 0.7 us  [dense_shards(): pl.pallas_call(store_kernel, out_shape=(jax.ShapeDtypeStruct(query_grad.s...]
where the time goes in v2:
time: 28.8 us; the launch traced here: 28.6 us
  Pallas kernels  28 us (97%)
  between operations  0.64 us (2%)
    pallas_call x1, Pallas kernels, dense_shards(): pl.pallas_call(functools.partial(dense_kernel, lines, planes, (local_quer...  27.3 us
    pallas_call x1, Pallas kernels, dense_shards(): pl.pallas_call(store_kernel, out_shape=(jax.ShapeDtypeStruct(query_grad.s...  0.7 us

profile of v2, /device:TPU:0, one launch (start us, length us, event | category | flops | bytes accessed | tf_op | source)
XLA Modules:
  0.0 28.6 jit_solution(13500434332097517514)
XLA Ops:
  0.6 27.3 %shard_map.77 = (bf16[256,128]{1,0:T(8,128)(2,1)S(1)}, bf16[512,128]{1,0:T(8,128)(2,1)S(1)}) custom-call(bf16[256,128]{1,0:T(8,128)(2,1)} %bitcast.9, bf16[2,512,128]{2,1,0:T(8,128)(2,1)} %bitcast.8, s32[1,64]{1,0:T(1,128)} %bitcast.10, s32[1,64]{1,0:T(1,128)} %bitcast.11, s32[1,64]{1,0:T(1,128)} %bitcast.12, s32[1,2]{1,0:T(1,128)} %bitcast.13), custom_call_target="tpu_custom_call" | custom-call | tf_op jit(solution)/shard_map/pallas_call | solution.py:400
  27.9 0.7 %shard_map.78 = (bf16[256,128]{1,0:T(8,128)(2,1)}, bf16[512,128]{1,0:T(8,128)(2,1)}) custom-call(bf16[256,128]{1,0:T(8,128)(2,1)S(1)} %get-tuple-element.6.query_ref, bf16[512,128]{1,0:T(8,128)(2,1)S(1)} %get-tuple-element.7.page_ref), custom_call_target="tpu_custom_call" | custom-call | tf_op jit(solution)/shard_map/pallas_call | solution.py:442

commit v3 on v2

--- a/solution.py
+++ b/solution.py
@@ -22,25 +22,25 @@
         ("send_tokens", 2),
         ("block", (0, 1), (1, 1)),
         ("tokens", 3),
-        ("block", (3, 1), (3, 0)),
         ("relayed", 2),
-        ("block", (0, 2), (1, 2), (3, 2)),
+        ("block", (3, 1), (3, 0), (0, 2), (1, 2), (3, 2)),
         ("page", 3),
         ("tokens", 2),
         ("block", (2, 1), (2, 2)),
         ("finish", 1),
         ("finish", 2),
         ("relayed", 3),
-        ("block", (3, 3), (2, 3)),
+        ("block", (3, 3), (1, 3)),
         ("line", 3),
+        ("line", 1),
         ("share", 1),
         ("share", 2),
-        ("block", (2, 0), (1, 3), (0, 3)),
+        ("block", (2, 3), (0, 3)),
         ("finish", 3),
+        ("block", (2, 0)),
         ("line", 2),
-        ("line", 1),
+        ("share", 3),
         ("finish", 0),
-        ("share", 3),
     )
 
 

time: 28.8 us -> 28.4 us (0.986)
  Pallas kernels: 28 us -> 27.6 us
    pallas_call x1, Pallas kernels: 27.3 us -> 26.9 us  [dense_shards(): pl.pallas_call(functools.partial(dense_kernel, lines, planes, (local_quer...]
where the time goes in v3:
time: 28.4 us; the launch traced here: 28.2 us
  Pallas kernels  27.6 us (97%)
  between operations  0.64 us (2%)
    pallas_call x1, Pallas kernels, dense_shards(): pl.pallas_call(functools.partial(dense_kernel, lines, planes, (local_quer...  26.9 us
    pallas_call x1, Pallas kernels, dense_shards(): pl.pallas_call(store_kernel, out_shape=(jax.ShapeDtypeStruct(query_grad.s...  0.7 us

profile of v3, /device:TPU:0, one launch (start us, length us, event | category | flops | bytes accessed | tf_op | source)
XLA Modules:
  0.0 28.2 jit_solution(7693331054278078489)
XLA Ops:
  0.6 26.9 %shard_map.77 = (bf16[256,128]{1,0:T(8,128)(2,1)S(1)}, bf16[512,128]{1,0:T(8,128)(2,1)S(1)}) custom-call(bf16[256,128]{1,0:T(8,128)(2,1)} %bitcast.9, bf16[2,512,128]{2,1,0:T(8,128)(2,1)} %bitcast.8, s32[1,64]{1,0:T(1,128)} %bitcast.10, s32[1,64]{1,0:T(1,128)} %bitcast.11, s32[1,64]{1,0:T(1,128)} %bitcast.12, s32[1,2]{1,0:T(1,128)} %bitcast.13), custom_call_target="tpu_custom_call" | custom-call | tf_op jit(solution)/shard_map/pallas_call | solution.py:400
  27.5 0.7 %shard_map.78 = (bf16[256,128]{1,0:T(8,128)(2,1)}, bf16[512,128]{1,0:T(8,128)(2,1)}) custom-call(bf16[256,128]{1,0:T(8,128)(2,1)S(1)} %get-tuple-element.6.query_ref, bf16[512,128]{1,0:T(8,128)(2,1)S(1)} %get-tuple-element.7.page_ref), custom_call_target="tpu_custom_call" | custom-call | tf_op jit(solution)/shard_map/pallas_call | solution.py:442

commit v4 on v3

--- a/solution.py
+++ b/solution.py
@@ -17,9 +17,9 @@
     return (
         ("tokens", 1),
         ("block", (1, 0)),
+        ("send_tokens", 2),
         ("page", 1),
         ("send_page", 3),
-        ("send_tokens", 2),
         ("block", (0, 1), (1, 1)),
         ("tokens", 3),
         ("relayed", 2),

time: 28.4 us -> 28.4 us (level)
  no operation moved by 1% of the time
where the time goes in v4:
time: 28.4 us; the launch traced here: 28.2 us
  Pallas kernels  27.6 us (97%)
  between operations  0.64 us (2%)
    pallas_call x1, Pallas kernels, dense_shards(): pl.pallas_call(functools.partial(dense_kernel, lines, planes, (local_quer...  26.9 us
    pallas_call x1, Pallas kernels, dense_shards(): pl.pallas_call(store_kernel, out_shape=(jax.ShapeDtypeStruct(query_grad.s...  0.7 us

profile of v4, /device:TPU:0, one launch (start us, length us, event | category | flops | bytes accessed | tf_op | source)
XLA Modules:
  0.0 28.2 jit_solution(9969008275825273412)
XLA Ops:
  0.6 26.9 %shard_map.77 = (bf16[256,128]{1,0:T(8,128)(2,1)S(1)}, bf16[512,128]{1,0:T(8,128)(2,1)S(1)}) custom-call(bf16[256,128]{1,0:T(8,128)(2,1)} %bitcast.9, bf16[2,512,128]{2,1,0:T(8,128)(2,1)} %bitcast.8, s32[1,64]{1,0:T(1,128)} %bitcast.10, s32[1,64]{1,0:T(1,128)} %bitcast.11, s32[1,64]{1,0:T(1,128)} %bitcast.12, s32[1,2]{1,0:T(1,128)} %bitcast.13), custom_call_target="tpu_custom_call" | custom-call | tf_op jit(solution)/shard_map/pallas_call | solution.py:400
  27.5 0.7 %shard_map.78 = (bf16[256,128]{1,0:T(8,128)(2,1)}, bf16[512,128]{1,0:T(8,128)(2,1)}) custom-call(bf16[256,128]{1,0:T(8,128)(2,1)S(1)} %get-tuple-element.6.query_ref, bf16[512,128]{1,0:T(8,128)(2,1)S(1)} %get-tuple-element.7.page_ref), custom_call_target="tpu_custom_call" | custom-call | tf_op jit(solution)/shard_map/pallas_call | solution.py:442

commit v5 on v4

--- a/solution.py
+++ b/solution.py
@@ -35,8 +35,7 @@
         ("line", 1),
         ("share", 1),
         ("share", 2),
-        ("block", (2, 3), (0, 3)),
-        ("finish", 3),
+        ("last", (2, 3), (0, 3)),
         ("block", (2, 0)),
         ("line", 2),
         ("share", 3),
@@ -292,6 +291,27 @@
             terms = by_page[:, side * part : (side + 1) * part]
             page_acc[plane, side] = terms if first_page else page_acc[plane, side] + terms
 
+    def last(*places):
+        spots = [(my_line ^ hop, turn(jump)) for hop, jump in places]
+        dots = [logits(*spot) for spot in spots]
+        final = [weights(dot, *spot) for spot, dot in zip(spots, dots)]
+        plane = spots[0][1]
+        for (line, _), weight in zip(spots, final):
+            by_page = lax.dot_general(
+                held[line, pl.ds(0, rows), :],
+                weight,
+                (((0,), (0,)), ((), ())),
+                preferred_element_type=jnp.float32,
+            )
+            for side in range(page_acc.shape[1]):
+                terms = by_page[:, side * part : (side + 1) * part]
+                page_acc[plane, side] = page_acc[plane, side] + terms
+        act("finish", places[0][1])
+        for (line, _), weight in zip(spots, final):
+            query_acc[line] += jnp.dot(
+                weight, paged[plane].reshape(patches, width), preferred_element_type=jnp.float32
+            )
+
     def block(*places):
         spots = [(my_line ^ hop, turn(jump)) for hop, jump in places]
         dots = [logits(*spot) for spot in spots]
@@ -308,6 +328,9 @@
     def act(kind, *what):
         if kind == "block":
             block(*what)
+            return
+        if kind == "last":
+            last(*what)
             return
         offset_by = what[0]
         line, plane = my_line ^ offset_by, turn(offset_by)

time: 28.4 us -> 28.4 us (level)
  no operation moved by 1% of the time
where the time goes in v5:
time: 28.4 us; the launch traced here: 28.2 us
  Pallas kernels  27.6 us (97%)
  between operations  0.64 us (2%)
    pallas_call x1, Pallas kernels, dense_shards(): pl.pallas_call(functools.partial(dense_kernel, lines, planes, (local_quer...  26.9 us
    pallas_call x1, Pallas kernels, dense_shards(): pl.pallas_call(store_kernel, out_shape=(jax.ShapeDtypeStruct(query_grad.s...  0.7 us

profile of v5, /device:TPU:0, one launch (start us, length us, event | category | flops | bytes accessed | tf_op | source)
XLA Modules:
  0.0 28.2 jit_solution(14305056449201408291)
XLA Ops:
  0.6 26.9 %shard_map.77 = (bf16[256,128]{1,0:T(8,128)(2,1)S(1)}, bf16[512,128]{1,0:T(8,128)(2,1)S(1)}) custom-call(bf16[256,128]{1,0:T(8,128)(2,1)} %bitcast.9, bf16[2,512,128]{2,1,0:T(8,128)(2,1)} %bitcast.8, s32[1,64]{1,0:T(1,128)} %bitcast.10, s32[1,64]{1,0:T(1,128)} %bitcast.11, s32[1,64]{1,0:T(1,128)} %bitcast.12, s32[1,2]{1,0:T(1,128)} %bitcast.13), custom_call_target="tpu_custom_call" | custom-call | tf_op jit(solution)/shard_map/pallas_call | solution.py:423
  27.5 0.7 %shard_map.78 = (bf16[256,128]{1,0:T(8,128)(2,1)}, bf16[512,128]{1,0:T(8,128)(2,1)}) custom-call(bf16[256,128]{1,0:T(8,128)(2,1)S(1)} %get-tuple-element.6.query_ref, bf16[512,128]{1,0:T(8,128)(2,1)S(1)} %get-tuple-element.7.page_ref), custom_call_target="tpu_custom_call" | custom-call | tf_op jit(solution)/shard_map/pallas_call | solution.py:465
